TPU v7x, 256 devices: a whole 4x4x8 slice. The times are simulated.
256 devices in a mesh: pipe: 16 (over z, core), dp: 4 (over x), tensor: 4 (over y).
Axes of the slice: x: 4, y: 4, z: 8, core: 2. Of those that a mesh axis runs over, the one named last changes fastest.
Arguments:
- acts: bfloat16 [16, 2048, 8192], P('pipe', 'dp', 'tensor'), may hold values from -6 to 6
- grads: bfloat16 [16, 2048, 8192], P('pipe', 'dp', 'tensor'), may hold values from -6 to 6
- sketch_index: int32 [16, 2, 16], P('pipe'), may hold values from 0 to 63, as said below
- sketch_values: bfloat16 [16, 2, 16, 128, 32], P('pipe'), may hold values from -0.125 to 0.125
Outputs:
- basis: float32 [16384, 256], P(('pipe', 'tensor'), 'dp')
Inputs may be any that keep to these rules, and one draw needn't show every extreme that they name: `sketch_index`: the 16 blocks of each sketch are distinct.
All inputs are finite; a program needn't handle non-finite values.
Results may differ from a plain program's by a relative error of at most 0.0003.
Values sent between devices are 32-bit elements; how exact they have to be, the bound alone decides.
A program may use at most 64 MiB of HBM per device.

v0:
```python
import jax
import jax.numpy as jnp
from jax import lax
from jax.sharding import PartitionSpec as P

RANK = 256
ITERS = 2
TOK_EX = 4


def mm(a, b):
    return jnp.matmul(a, b, precision=lax.Precision.HIGHEST)


def mm_tn(a, b):
    return lax.dot_general(a, b, (((0,), (0,)), ((), ())), precision=lax.Precision.HIGHEST)


def solve_lower_t(lower, block):
    return lax.linalg.triangular_solve(lower, block, left_side=False, lower=True, transpose_a=True)


def merged_coords(gram):
    cols = gram.shape[0]
    eye = jnp.eye(RANK, dtype=gram.dtype)
    pick = jnp.concatenate([eye] * (cols // RANK), axis=0)
    lower = jnp.linalg.cholesky(mm_tn(pick, mm(gram, pick)))
    coords = solve_lower_t(lower, pick)
    for turn in range(ITERS):
        image = mm(gram, coords)
        lower = jnp.linalg.cholesky(mm_tn(image, mm(gram, image)))
        coords = solve_lower_t(lower, image)
    weights = mm(gram, coords)
    lower = jnp.linalg.cholesky(mm_tn(weights, weights))
    return mm(coords, lower)


def shards(acts, grads, sketch_index, sketch_values):
    local_width = acts.shape[2]
    blocks = local_width // 128
    width = sketch_values.shape[4]
    tensor_pos = lax.axis_index("tensor")
    tensor_count = lax.axis_size("tensor")
    dp_pos = lax.axis_index("dp")
    dp_count = lax.axis_size("dp")
    span = jnp.arange(blocks, dtype=jnp.int32) + tensor_pos * blocks
    onehot = (sketch_index[0][:, :, None] == span[None, None, :]).astype(jnp.bfloat16)
    local = jnp.einsum(
        "sij,sicd->sjcd", onehot, sketch_values[0], preferred_element_type=jnp.float32
    )
    local = local.astype(jnp.bfloat16).reshape(2, local_width, width)
    left_part = jnp.dot(acts[0], local[0], preferred_element_type=jnp.float32)
    right_part = jnp.dot(grads[0], local[1], preferred_element_type=jnp.float32)
    both = lax.psum(jnp.concatenate([left_part, right_part], axis=1), "tensor")
    both = lax.all_gather(both, "dp", axis=0, tiled=True)
    left_all = both[:, :width].reshape(-1, TOK_EX, width)
    right_all = both[:, width:].reshape(-1, TOK_EX, width)
    outer = jnp.einsum("etk,etl->ekl", left_all, right_all, precision=lax.Precision.HIGHEST)
    joined_t = outer.reshape(outer.shape[0], -1)
    gram = lax.psum(mm(joined_t, joined_t.T), "pipe")
    coords = merged_coords(gram)
    part_rows = joined_t.shape[1] // tensor_count
    rows = lax.dynamic_slice_in_dim(joined_t, tensor_pos * part_rows, part_rows, 1)
    own_columns = coords.shape[1] // dp_count
    coords = lax.dynamic_slice_in_dim(coords, dp_pos * own_columns, own_columns, 1)
    return mm_tn(rows, coords)


def solution(mesh):
    placed = (
        P("pipe", "dp", "tensor"),
        P("pipe", "dp", "tensor"),
        P("pipe", None, None),
        P("pipe", None, None, None, None),
    )
    return jax.shard_map(
        shards, mesh=mesh, in_specs=placed, out_specs=P(("pipe", "tensor"), "dp"), check_vma=False
    )
```

profile of v0, /device:TPU:1, one launch (start us, length us, event | category | flops | bytes accessed | tf_op | source)
XLA Modules:
  0.0 487.8 jit_solution(8322790528402684456)
XLA Ops:
  6.5 1.4 convolution_convert_fusion
  10.4 48.4 %all-reduce.4.cloned.1.call-done = f32[512,64]{0,1:T(8,128)} async-done(((f32[512,64]{0,1:T(8,128)}), f32[512,64]{0,1:T(8,128)}) %all-reduce.4.cloned.1.call-update) | async-done | bytes 131088 | tf_op jit(solution)/shard_map/psum | solution.py:54
  58.8 10.5 %all_gather.3 = f32[2048,64]{0,1:T(8,128)S(1)} all-gather(f32[512,64]{0,1:T(8,128)} %all-reduce.4.cloned.1.call-done), channel_id=1, replica_groups=mesh['pipe'=16,'dp'=4,'tensor'=4] {'dp'}, dimensions={0}, use_global_device_ids=true | all-gather | bytes 655360 | tf_op jit(solution)/shard_map/all_gather | solution.py:55
  70.1 1.3 copy.15
  71.4 1.4 copy.16
  72.8 16.5 %fusion.90 = f32[512,32,32]{2,1,0:T(8,128)} fusion(f32[512,4,32]{2,1,0:T(4,128)S(1)} %bitcast.168, f32[512,4,32]{2,1,0:T(4,128)} %bitcast.169), kind=kOutput, calls=%fused_computation.147 | convolution fusion | flops 25165824 | bytes 2621440 | tf_op jit(solution)/shard_map/etk,etl->ekl/dot_general | solution.py:58
  89.2 6.4 %copy.17 = f32[512,32,32]{0,2,1:T(8,128)} copy(f32[512,32,32]{2,1,0:T(8,128)} %fusion.90) | data formatting | bytes 4194304 | tf_op jit(solution)/shard_map/etk,etl->ekl/dot_general | solution.py:58
  95.7 6.8 %convolution_bitcast_fusion = f32[512,512]{1,0:T(8,128)} fusion(f32[512,32,32]{0,2,1:T(8,128)} %copy.17), kind=kOutput, calls=%fused_computation.10 | convolution fusion | flops 3221225472 | bytes 3145728 | tf_op jit(solution)/shard_map/dot_general | solution.py:12
  103.4 116.2 %all-reduce.6.cloned.1.call-done = f32[512,512]{1,0:T(8,128)} async-done(((f32[512,512]{1,0:T(8,128)}), f32[512,512]{1,0:T(8,128)}) %all-reduce.6.cloned.1.call-update) | async-done | bytes 1048592 | tf_op jit(solution)/shard_map/psum | solution.py:60
  219.6 1.8 fusion.70
  223.0 11.7 %cholesky.214 = f32[128,128]{1,0:T(8,128)S(1)} custom-call(f32[128,128]{1,0:T(8,128)S(1)} %cholesky.346), custom_call_target="Cholesky" | custom-call | tf_op jit(solution)/shard_map/jit(cholesky)/cholesky | solution.py:27
  234.7 9.8 %custom-call.16 = f32[1,128,128]{1,2,0:T(8,128)S(1)} custom-call(f32[1,128,128]{2,1,0:T(8,128)S(1)} %get-tuple-element.79), custom_call_target="InvertDiagBlocksLowerTriangular" | custom-call | tf_op jit(solution)/shard_map/jit(cholesky)/cholesky | solution.py:27
  244.6 1.1 constant_dynamic-update-slice_fusion.7
  245.7 1.1 convolution_subtract_fusion.6
  246.8 12.1 %cholesky.231 = f32[128,128]{1,0:T(8,128)S(1)} custom-call(f32[128,128]{1,0:T(8,128)S(1)} %convolution_subtract_fusion.6), custom_call_target="Cholesky" | custom-call | tf_op jit(solution)/shard_map/jit(cholesky)/cholesky | solution.py:27
  262.0 4.1 while.6
  262.7 1.3 bitcast_dynamic-update-slice_fusion.6
  264.7 1.3 bitcast_dynamic-update-slice_fusion.6
  266.7 20.5 %custom-call.17 = f32[2,128,128]{1,2,0:T(8,128)S(1)} custom-call(f32[2,128,128]{2,1,0:T(8,128)} %copy-done.14), custom_call_target="InvertDiagBlocksLowerTriangular" | custom-call | tf_op jit(solution)/shard_map/triangular_solve/custom-call.0 | solution.py:20
  287.2 1.4 fusion.26
  288.6 1.5 convolution_subtract_fusion.2
  296.2 11.7 %cholesky.248 = f32[128,128]{1,0:T(8,128)S(1)} custom-call(f32[128,128]{1,0:T(8,128)S(1)} %cholesky.349), custom_call_target="Cholesky" | custom-call | tf_op jit(solution)/shard_map/jit(cholesky)/cholesky | solution.py:31
  307.9 9.8 %custom-call.18 = f32[1,128,128]{1,2,0:T(8,128)S(1)} custom-call(f32[1,128,128]{2,1,0:T(8,128)S(1)} %get-tuple-element.75), custom_call_target="InvertDiagBlocksLowerTriangular" | custom-call | tf_op jit(solution)/shard_map/jit(cholesky)/cholesky | solution.py:31
  317.7 1.0 constant_dynamic-update-slice_fusion.5
  318.8 1.1 convolution_subtract_fusion.5
  319.9 11.9 %cholesky.265 = f32[128,128]{1,0:T(8,128)S(1)} custom-call(f32[128,128]{1,0:T(8,128)S(1)} %convolution_subtract_fusion.5), custom_call_target="Cholesky" | custom-call | tf_op jit(solution)/shard_map/jit(cholesky)/cholesky | solution.py:31
  335.4 4.1 while.7
  336.1 1.4 bitcast_dynamic-update-slice_fusion.7
  338.1 1.4 bitcast_dynamic-update-slice_fusion.7
  340.2 20.5 %custom-call.19 = f32[2,128,128]{1,2,0:T(8,128)S(1)} custom-call(f32[2,128,128]{2,1,0:T(8,128)} %copy-done.15), custom_call_target="InvertDiagBlocksLowerTriangular" | custom-call | tf_op jit(solution)/shard_map/triangular_solve/custom-call.0 | solution.py:20
  360.7 1.4 fusion.24
  362.1 1.5 convolution_subtract_fusion.1
  364.1 1.0 fusion.14
  369.6 11.7 %cholesky.282 = f32[128,128]{1,0:T(8,128)S(1)} custom-call(f32[128,128]{1,0:T(8,128)S(1)} %cholesky.352), custom_call_target="Cholesky" | custom-call | tf_op jit(solution)/shard_map/jit(cholesky)/cholesky | solution.py:31
  381.4 9.8 %custom-call.20 = f32[1,128,128]{1,2,0:T(8,128)S(1)} custom-call(f32[1,128,128]{2,1,0:T(8,128)S(1)} %get-tuple-element.71), custom_call_target="InvertDiagBlocksLowerTriangular" | custom-call | tf_op jit(solution)/shard_map/jit(cholesky)/cholesky | solution.py:31
  391.2 1.0 constant_dynamic-update-slice_fusion.2
  392.3 1.1 convolution_subtract_fusion.4
  393.4 12.1 %cholesky.299 = f32[128,128]{1,0:T(8,128)S(1)} custom-call(f32[128,128]{1,0:T(8,128)S(1)} %convolution_subtract_fusion.4), custom_call_target="Cholesky" | custom-call | tf_op jit(solution)/shard_map/jit(cholesky)/cholesky | solution.py:31
  409.2 4.1 while.8
  409.8 1.4 bitcast_dynamic-update-slice_fusion.8
  411.8 1.4 bitcast_dynamic-update-slice_fusion.8
  414.6 20.5 %custom-call.21 = f32[2,128,128]{1,2,0:T(8,128)S(1)} custom-call(f32[2,128,128]{2,1,0:T(8,128)} %copy-done.16), custom_call_target="InvertDiagBlocksLowerTriangular" | custom-call | tf_op jit(solution)/shard_map/triangular_solve/custom-call.0 | solution.py:20
  435.1 1.4 fusion.22
  436.5 1.6 convolution_subtract_fusion
  440.8 11.7 %cholesky.316 = f32[128,128]{1,0:T(8,128)S(1)} custom-call(f32[128,128]{1,0:T(8,128)S(1)} %cholesky.355), custom_call_target="Cholesky" | custom-call | tf_op jit(solution)/shard_map/jit(cholesky)/cholesky | solution.py:34
  452.6 9.8 %custom-call.22 = f32[1,128,128]{1,2,0:T(8,128)S(1)} custom-call(f32[1,128,128]{2,1,0:T(8,128)S(1)} %get-tuple-element.67), custom_call_target="InvertDiagBlocksLowerTriangular" | custom-call | tf_op jit(solution)/shard_map/jit(cholesky)/cholesky | solution.py:34
  462.9 11.9 %cholesky.333 = f32[128,128]{1,0:T(8,128)S(1)} custom-call(f32[128,128]{1,0:T(8,128)S(1)} %convolution_subtract_fusion.3), custom_call_target="Cholesky" | custom-call | tf_op jit(solution)/shard_map/jit(cholesky)/cholesky | solution.py:34
  478.4 2.4 fusion.18
  (111 shorter events, 35.0 us)
Async XLA Ops:
  6.5 1.7 copy-start
  6.5 52.3 %all-reduce.4.cloned.1.call-start = ((), (), s32[]{:S(2)}) async-start(), calls=%async_computation | async-start | bytes 262144 | tf_op jit(solution)/shard_map/psum | solution.py:54
  6.5 2.4 copy-start.6
  10.4 209.2 %all-reduce.6.cloned.1.call-start = ((), (), s32[]{:S(2)}) async-start(), calls=%async_computation.1 | async-start | bytes 2097152 | tf_op jit(solution)/shard_map/psum | solution.py:60
  222.3 0.7 copy-start.11
  244.6 46.0 %copy-start.1 = (f32[512,512]{1,0:T(8,128)S(1)}, f32[512,512]{1,0:T(8,128)}, u32[]{:S(2)}) copy-start(f32[512,512]{1,0:T(8,128)} %all-reduce.6.cloned.1.call-done) | copy-start | bytes 3145732
  259.0 1.9 copy-start.10
  266.1 0.6 copy-start.14
  291.6 1.0 copy-start.3
  295.4 0.7 copy-start.12
  331.8 2.6 copy-start.8
  339.6 0.7 copy-start.15
  365.1 1.0 copy-start.2
  368.9 0.7 copy-start.13
  405.5 2.6 copy-start.9
  413.3 0.7 copy-start.16
  413.9 0.7 copy-start.7
  438.5 1.0 copy-start.4
  440.6 36.8 %copy-start.5 = (f32[512,128]{0,1:T(8,128)S(1)}, f32[512,128]{0,1:T(8,128)}, u32[]{:S(2)}) copy-start(f32[512,128]{0,1:T(8,128)} %copy-done.4) | copy-start | bytes 786436
Sparse Core Ops, SparseCore 0:
  10.5 48.2 all-reduce.3
  102.6 116.9 all-reduce.5
where the time goes:
time: 496 us; the launch traced here: 488 us
  other arithmetic  207 us (42%)
  waiting for transfers between devices  165 us (33%)
  matrix products  57 us (11%)
  local copies, waits for them, and re-layouts  29.2 us (6%)
  between operations  19.3 us (4%)
  blocking collectives  10.5 us (2%)
    psum x1, waiting for transfers between devices, shards(): gram = lax.psum(mm(joined_t, joined_t.T), 'pipe')  116 us
    another operation x14, other arithmetic, merged_coords(): lower = jnp.linalg.cholesky(mm_tn(image, mm(gram, image)))  69.8 us
    another operation x7, other arithmetic, solve_lower_t(): lax.linalg.triangular_solve(lower, block, left_side=False, lower=True, tr...  64.4 us
    psum x1, waiting for transfers between devices, shards(): both = lax.psum(jnp.concatenate([left_part, right_part], axis=1), 'tensor')  48.4 us
    another operation x7, other arithmetic, merged_coords(): lower = jnp.linalg.cholesky(mm_tn(weights, weights))  34.8 us
    another operation x6, other arithmetic, merged_coords(): lower = jnp.linalg.cholesky(mm_tn(pick, mm(gram, pick)))  34.4 us
    dot_general x1, matrix products, shards(): jnp.einsum('etk,etl->ekl', left_all, right_all, precision=lax.Precision.H...  16.5 us
    dot_general x8, matrix products, mm(): return jnp.matmul(a, b, precision=lax.Precision.HIGHEST)  14.7 us
  transfers between devices with their start and end apart: 2, of which 2 were waited for; matrix products, arithmetic and copies ran while one was open for 0% of the time, Pallas kernels for 0%

commit v1 on v0

--- a/solution.py
+++ b/solution.py
@@ -57,7 +57,8 @@
     right_all = both[:, width:].reshape(-1, TOK_EX, width)
     outer = jnp.einsum("etk,etl->ekl", left_all, right_all, precision=lax.Precision.HIGHEST)
     joined_t = outer.reshape(outer.shape[0], -1)
-    gram = lax.psum(mm(joined_t, joined_t.T), "pipe")
+    local_values = mm(joined_t, joined_t.T)
+    gram = jnp.sum(lax.all_gather(local_values, axis_name="pipe"), axis=0)
     coords = merged_coords(gram)
     part_rows = joined_t.shape[1] // tensor_count
     rows = lax.dynamic_slice_in_dim(joined_t, tensor_pos * part_rows, part_rows, 1)

time: 496 us -> 487 us (0.982)
  waiting for transfers between devices: 165 us -> 148 us
  other arithmetic: 207 us -> 216 us
    psum x1 -> x0, waiting for transfers between devices: 116 us -> none  [shards(): gram = lax.psum(mm(joined_t, joined_t.T), 'pipe')]
    all_gather x0 -> x1, waiting for transfers between devices: none -> 99.7 us  [shards(): gram = jnp.sum(lax.all_gather(local_values, axis_name='pipe'), axis=0)]
    reduce_sum x0 -> x1, other arithmetic: none -> 7.91 us  [shards(): gram = jnp.sum(lax.all_gather(local_values, axis_name='pipe'), axis=0)]
where the time goes in v1:
time: 487 us; the launch traced here: 479 us
  other arithmetic  216 us (44%)
  waiting for transfers between devices  148 us (30%)
  matrix products  55.6 us (11%)
  local copies, waits for them, and re-layouts  29.4 us (6%)
  between operations  19.2 us (4%)
  blocking collectives  10.5 us (2%)
    all_gather x1, waiting for transfers between devices, shards(): gram = jnp.sum(lax.all_gather(local_values, axis_name='pipe'), axis=0)  99.7 us
    another operation x14, other arithmetic, merged_coords(): lower = jnp.linalg.cholesky(mm_tn(image, mm(gram, image)))  69.7 us
    another operation x7, other arithmetic, solve_lower_t(): lax.linalg.triangular_solve(lower, block, left_side=False, lower=True, tr...  64.9 us
    psum x1, waiting for transfers between devices, shards(): both = lax.psum(jnp.concatenate([left_part, right_part], axis=1), 'tensor')  48.4 us
    another operation x7, other arithmetic, merged_coords(): lower = jnp.linalg.cholesky(mm_tn(weights, weights))  34.8 us
    another operation x6, other arithmetic, merged_coords(): lower = jnp.linalg.cholesky(mm_tn(pick, mm(gram, pick)))  34.1 us
    dot_general x1, matrix products, shards(): jnp.einsum('etk,etl->ekl', left_all, right_all, precision=lax.Precision.H...  16.5 us
    dot_general x8, matrix products, mm(): return jnp.matmul(a, b, precision=lax.Precision.HIGHEST)  13.4 us
  transfers between devices with their start and end apart: 2, of which 2 were waited for; matrix products, arithmetic and copies ran while one was open for 0% of the time, Pallas kernels for 0%

profile of v1, /device:TPU:1, one launch (start us, length us, event | category | flops | bytes accessed | tf_op | source)
XLA Modules:
  0.0 479.0 jit_solution(6050604153519101934)
XLA Ops:
  6.5 1.4 convolution_convert_fusion
  10.4 48.4 %all-reduce.3.cloned.1.call-done = f32[512,64]{0,1:T(8,128)} async-done(((f32[512,64]{0,1:T(8,128)}), f32[512,64]{0,1:T(8,128)}) %all-reduce.3.cloned.1.call-update) | async-done | bytes 131088 | tf_op jit(solution)/shard_map/psum | solution.py:54
  58.8 10.5 %all_gather.9 = f32[2048,64]{0,1:T(8,128)S(1)} all-gather(f32[512,64]{0,1:T(8,128)} %all-reduce.3.cloned.1.call-done), channel_id=1, replica_groups=mesh['pipe'=16,'dp'=4,'tensor'=4] {'dp'}, dimensions={0}, use_global_device_ids=true | all-gather | bytes 655360 | tf_op jit(solution)/shard_map/all_gather | solution.py:55
  70.1 1.3 copy.15
  71.4 1.4 copy.16
  72.8 16.5 %fusion.90 = f32[512,32,32]{2,1,0:T(8,128)} fusion(f32[512,4,32]{2,1,0:T(4,128)S(1)} %bitcast.170, f32[512,4,32]{2,1,0:T(4,128)} %bitcast.171), kind=kOutput, calls=%fused_computation.147 | convolution fusion | flops 25165824 | bytes 2621440 | tf_op jit(solution)/shard_map/etk,etl->ekl/dot_general | solution.py:58
  89.2 6.4 %copy.17 = f32[512,32,32]{0,2,1:T(8,128)} copy(f32[512,32,32]{2,1,0:T(8,128)} %fusion.90) | data formatting | bytes 4194304 | tf_op jit(solution)/shard_map/etk,etl->ekl/dot_general | solution.py:58
  95.7 6.7 %convolution_bitcast_fusion = f32[512,512]{1,0:T(8,128)} fusion(f32[512,32,32]{0,2,1:T(8,128)} %copy.17), kind=kOutput, calls=%fused_computation.10 | convolution fusion | flops 3221225472 | bytes 3145728 | tf_op jit(solution)/shard_map/dot_general | solution.py:12
  103.3 99.7 %all-gather.3.cloned.1.call-done = f32[8192,512]{1,0:T(8,128)} async-done(((f32[512,512]{1,0:T(8,128)}), f32[8192,512]{1,0:T(8,128)}) %all-gather.3.cloned.1.call-update) | async-done | bytes 16777232 | tf_op jit(solution)/shard_map/all_gather | solution.py:61
  203.0 7.9 %reduce_sum.9 = f32[512,512]{1,0:T(8,128)S(1)} reduce(f32[16,512,512]{2,1,0:T(8,128)} %bitcast.169, f32[]{:T(128)} %constant.71.clone.1), dimensions={0}, to_apply=%region_1.0 | reduce | flops 3932160 | bytes 17825796 | tf_op jit(solution)/shard_map/reduce_sum | solution.py:61
  214.7 11.7 %cholesky.214 = f32[128,128]{1,0:T(8,128)S(1)} custom-call(f32[128,128]{1,0:T(8,128)S(1)} %cholesky.346), custom_call_target="Cholesky" | custom-call | tf_op jit(solution)/shard_map/jit(cholesky)/cholesky | solution.py:27
  226.5 10.0 %custom-call.16 = f32[1,128,128]{1,2,0:T(8,128)S(1)} custom-call(f32[1,128,128]{2,1,0:T(8,128)S(1)} %get-tuple-element.79), custom_call_target="InvertDiagBlocksLowerTriangular" | custom-call | tf_op jit(solution)/shard_map/jit(cholesky)/cholesky | solution.py:27
  236.5 1.0 constant_dynamic-update-slice_fusion.7
  237.6 1.1 convolution_subtract_fusion.6
  238.7 11.7 %cholesky.231 = f32[128,128]{1,0:T(8,128)S(1)} custom-call(f32[128,128]{1,0:T(8,128)S(1)} %convolution_subtract_fusion.6), custom_call_target="Cholesky" | custom-call | tf_op jit(solution)/shard_map/jit(cholesky)/cholesky | solution.py:27
  253.4 3.9 while.6
  254.0 1.3 bitcast_dynamic-update-slice_fusion.6
  256.0 1.3 bitcast_dynamic-update-slice_fusion.6
  257.9 20.9 %custom-call.17 = f32[2,128,128]{1,2,0:T(8,128)S(1)} custom-call(f32[2,128,128]{2,1,0:T(8,128)} %copy-done.13), custom_call_target="InvertDiagBlocksLowerTriangular" | custom-call | tf_op jit(solution)/shard_map/triangular_solve/custom-call.0 | solution.py:20
  278.9 1.4 fusion.26
  280.3 1.5 convolution_subtract_fusion.2
  287.8 11.7 %cholesky.248 = f32[128,128]{1,0:T(8,128)S(1)} custom-call(f32[128,128]{1,0:T(8,128)S(1)} %cholesky.349), custom_call_target="Cholesky" | custom-call | tf_op jit(solution)/shard_map/jit(cholesky)/cholesky | solution.py:31
  299.6 9.8 %custom-call.18 = f32[1,128,128]{1,2,0:T(8,128)S(1)} custom-call(f32[1,128,128]{2,1,0:T(8,128)S(1)} %get-tuple-element.75), custom_call_target="InvertDiagBlocksLowerTriangular" | custom-call | tf_op jit(solution)/shard_map/jit(cholesky)/cholesky | solution.py:31
  309.4 1.0 constant_dynamic-update-slice_fusion.5
  310.5 1.1 convolution_subtract_fusion.5
  311.6 11.9 %cholesky.265 = f32[128,128]{1,0:T(8,128)S(1)} custom-call(f32[128,128]{1,0:T(8,128)S(1)} %convolution_subtract_fusion.5), custom_call_target="Cholesky" | custom-call | tf_op jit(solution)/shard_map/jit(cholesky)/cholesky | solution.py:31
  327.1 3.9 while.7
  327.7 1.3 bitcast_dynamic-update-slice_fusion.7
  329.6 1.3 bitcast_dynamic-update-slice_fusion.7
  331.7 20.5 %custom-call.19 = f32[2,128,128]{1,2,0:T(8,128)S(1)} custom-call(f32[2,128,128]{2,1,0:T(8,128)} %copy-done.14), custom_call_target="InvertDiagBlocksLowerTriangular" | custom-call | tf_op jit(solution)/shard_map/triangular_solve/custom-call.0 | solution.py:20
  352.1 1.4 fusion.24
  353.5 1.5 convolution_subtract_fusion.1
  355.5 1.0 fusion.14
  361.1 11.7 %cholesky.282 = f32[128,128]{1,0:T(8,128)S(1)} custom-call(f32[128,128]{1,0:T(8,128)S(1)} %cholesky.352), custom_call_target="Cholesky" | custom-call | tf_op jit(solution)/shard_map/jit(cholesky)/cholesky | solution.py:31
  372.9 9.8 %custom-call.20 = f32[1,128,128]{1,2,0:T(8,128)S(1)} custom-call(f32[1,128,128]{2,1,0:T(8,128)S(1)} %get-tuple-element.71), custom_call_target="InvertDiagBlocksLowerTriangular" | custom-call | tf_op jit(solution)/shard_map/jit(cholesky)/cholesky | solution.py:31
  382.7 1.0 constant_dynamic-update-slice_fusion.2
  383.7 1.1 convolution_subtract_fusion.4
  384.8 12.1 %cholesky.299 = f32[128,128]{1,0:T(8,128)S(1)} custom-call(f32[128,128]{1,0:T(8,128)S(1)} %convolution_subtract_fusion.4), custom_call_target="Cholesky" | custom-call | tf_op jit(solution)/shard_map/jit(cholesky)/cholesky | solution.py:31
  400.5 3.9 while.8
  401.1 1.3 bitcast_dynamic-update-slice_fusion.8
  403.1 1.3 bitcast_dynamic-update-slice_fusion.8
  405.8 20.5 %custom-call.21 = f32[2,128,128]{1,2,0:T(8,128)S(1)} custom-call(f32[2,128,128]{2,1,0:T(8,128)} %copy-done.15), custom_call_target="InvertDiagBlocksLowerTriangular" | custom-call | tf_op jit(solution)/shard_map/triangular_solve/custom-call.0 | solution.py:20
  426.3 1.4 fusion.22
  427.7 1.6 convolution_subtract_fusion
  432.0 11.7 %cholesky.316 = f32[128,128]{1,0:T(8,128)S(1)} custom-call(f32[128,128]{1,0:T(8,128)S(1)} %cholesky.355), custom_call_target="Cholesky" | custom-call | tf_op jit(solution)/shard_map/jit(cholesky)/cholesky | solution.py:34
  443.8 9.8 %custom-call.22 = f32[1,128,128]{1,2,0:T(8,128)S(1)} custom-call(f32[1,128,128]{2,1,0:T(8,128)S(1)} %get-tuple-element.67), custom_call_target="InvertDiagBlocksLowerTriangular" | custom-call | tf_op jit(solution)/shard_map/jit(cholesky)/cholesky | solution.py:34
  454.1 11.9 %cholesky.333 = f32[128,128]{1,0:T(8,128)S(1)} custom-call(f32[128,128]{1,0:T(8,128)S(1)} %convolution_subtract_fusion.3), custom_call_target="Cholesky" | custom-call | tf_op jit(solution)/shard_map/jit(cholesky)/cholesky | solution.py:34
  469.6 2.4 fusion.18
  (110 shorter events, 37.1 us)
Async XLA Ops:
  6.5 1.7 copy-start
  6.5 52.3 %all-reduce.3.cloned.1.call-start = ((), (), s32[]{:S(2)}) async-start(), calls=%async_computation | async-start | bytes 262144 | tf_op jit(solution)/shard_map/psum | solution.py:54
  6.5 2.4 copy-start.5
  10.4 192.6 %all-gather.3.cloned.1.call-start = ((), (), s32[]{:S(2)}) async-start(), calls=%async_computation.1 | async-start | bytes 17825792 | tf_op jit(solution)/shard_map/all_gather | solution.py:61
  214.0 0.7 copy-start.10
  250.4 1.9 copy-start.9
  257.3 0.6 copy-start.13
  283.3 1.0 copy-start.2
  287.1 0.7 copy-start.11
  323.5 2.6 copy-start.7
  331.0 0.7 copy-start.14
  356.5 1.0 copy-start.1
  360.4 0.7 copy-start.12
  397.0 2.6 copy-start.8
  404.5 0.7 copy-start.15
  405.1 0.7 copy-start.6
  429.7 1.0 copy-start.3
  431.8 36.8 %copy-start.4 = (f32[512,128]{0,1:T(8,128)S(1)}, f32[512,128]{0,1:T(8,128)}, u32[]{:S(2)}) copy-start(f32[512,128]{0,1:T(8,128)} %copy-done.3) | copy-start | bytes 786436
Sparse Core Ops, SparseCore 0:
  10.5 48.2 all-reduce.2
  102.5 100.4 all-gather.2
